TPU v7x, 32 devices: a whole 2x2x4 slice. The times are simulated.
32 devices in a mesh: energy: 2 (over x), mom: 16 (over z, y, core).
Axes of the slice: x: 2, y: 2, z: 4, core: 2. Of those that a mesh axis runs over, the one named last changes fastest.
Arguments:
- source: float32 [256, 128, 1024], P(('energy', 'mom')), parts along dimension 0, may hold values from -6 to 6
- green: float32 [256, 1024], P(('energy', 'mom')), parts along dimension 0, may hold values from 0.1 to 0.6
- couple_one: float32 [2, 4, 128, 128], replicated, may hold values from -0.5 to 0.5
- couple_two: float32 [2, 4, 128, 128], replicated, may hold values from -0.5 to 0.5
- p_bracket: int32 [2, 1024], replicated, may hold values from 0 to 28
- q_bracket: int32 [2, 1024], replicated, may hold values from 0 to 28
- p_weight: float32 [2, 4, 1024], replicated, may hold values from -0.25 to 1
- q_weight: float32 [2, 4, 1024], replicated, may hold values from -0.25 to 1
- qr_bracket: int32 [2, 1024], replicated, may hold values from 0 to 28
- r_bracket: int32 [2, 1024], replicated, may hold values from 0 to 28
- qr_weight: float32 [2, 4, 1024], replicated, may hold values from -0.25 to 1
- r_weight: float32 [2, 4, 1024], replicated, may hold values from -0.25 to 1
Outputs:
- amplitude: float32 [256, 128, 1024], P(('energy', 'mom')), parts along dimension 0
- component: float32 [256, 128, 1024], P(('energy', 'mom')), parts along dimension 0
There are 2 independent parts, one for each index of `energy`. A program takes and returns all parts, laid end to end along the dimension named above; an argument that names none is the same for every part. Nothing has to cross between parts.
All inputs are finite; a program needn't handle non-finite values.
Results may differ from a plain program's by a relative error of at most 0.0001.
Values sent between devices are 32-bit elements; how exact they have to be, the bound alone decides.
No kernel may reach another device: no remote copies, remote signals or barrier semaphores. Data moves between devices by JAX's collectives and lax.ppermute only.
A program may use at most 128 MiB of HBM per device.

v0:
```python
import jax
import jax.numpy as jnp
from jax import lax
from jax.sharding import PartitionSpec as P

P_SIZE = 32
Q = 32
R = 32
K = 2
ITERS = 2


def spline_matrix(
    first_index, second_index, first_weight, second_weight, first_count, second_count
):
    first_grid = jnp.arange(first_count, dtype=jnp.int32)[None, :] - first_index[:, None]
    second_grid = jnp.arange(second_count, dtype=jnp.int32)[None, :] - second_index[:, None]
    first_rows = jnp.zeros(first_grid.shape, jnp.float32)
    second_rows = jnp.zeros(second_grid.shape, jnp.float32)
    for offset in range(4):
        first_rows = first_rows + jnp.where(
            first_grid == offset, first_weight[offset][:, None], jnp.float32(0.0)
        )
        second_rows = second_rows + jnp.where(
            second_grid == offset, second_weight[offset][:, None], jnp.float32(0.0)
        )
    return (first_rows[:, :, None] * second_rows[:, None, :]).reshape(
        first_index.shape[0], first_count * second_count
    )


def class_mats(couple, row_count, start):
    classes = (start + jnp.arange(row_count, dtype=jnp.int32)) % 4
    select = jax.nn.one_hot(classes, 4, dtype=jnp.float32)
    return jnp.einsum("rc,cmn->rmn", select, couple, precision=lax.Precision.HIGHEST)


def mix(mats, values):
    return jnp.einsum("rmn,rnx->rmx", mats, values, precision=lax.Precision.HIGHEST)


def interp(values, smat):
    return jnp.einsum("rcx,yx->rcy", values, smat, precision=lax.Precision.HIGHEST)


def to_send_one(values, quarter):
    rows = values.shape[0]
    return (
        values.reshape(rows, 4, quarter, P_SIZE, Q)
        .transpose(3, 1, 0, 2, 4)
        .reshape(4 * P_SIZE, rows, quarter * Q)
    )


def from_send_one(arrived, quarter):
    rows = arrived.shape[0]
    return (
        arrived.reshape(rows, R, 4, quarter, Q)
        .transpose(0, 3, 2, 4, 1)
        .reshape(rows, 4 * quarter, Q * R)
    )


def to_send_two(values, quarter):
    rows = values.shape[0]
    return (
        values.reshape(rows, quarter, 4, Q, R)
        .transpose(4, 2, 0, 1, 3)
        .reshape(4 * R, rows, quarter * Q)
    )


def from_send_two(arrived, quarter):
    rows = arrived.shape[0]
    return (
        arrived.reshape(rows, P_SIZE, 4, quarter, Q)
        .transpose(0, 2, 3, 1, 4)
        .reshape(rows, 4 * quarter, P_SIZE * Q)
    )


def shards(
    source,
    green,
    couple_one,
    couple_two,
    p_bracket,
    q_bracket,
    p_weight,
    q_weight,
    qr_bracket,
    r_bracket,
    qr_weight,
    r_weight,
):
    rows_one = source.shape[0]
    rows_two = green.shape[0]
    quarter = source.shape[1] // 4
    here = lax.axis_index("mom")
    first_maps = [
        spline_matrix(p_bracket[k], q_bracket[k], p_weight[k], q_weight[k], P_SIZE, Q)
        for k in range(K)
    ]
    second_maps = [
        spline_matrix(qr_bracket[k], r_bracket[k], qr_weight[k], r_weight[k], Q, R)
        for k in range(K)
    ]
    mats_one = [class_mats(couple_one[k], rows_one, here * rows_one) for k in range(K)]
    mats_two = [class_mats(couple_two[k], rows_two, here * rows_two) for k in range(K)]
    scale = green[:, None, :]
    state = source
    component = None
    for step in range(ITERS):
        one = interp(mix(mats_one[0], state), first_maps[0])
        k = 1
        one = one + interp(mix(mats_one[k], state), first_maps[k])
        arrived = lax.all_to_all(
            to_send_one(one, quarter), "mom", split_axis=0, concat_axis=1, tiled=True
        )
        regrouped = from_send_one(arrived, quarter)
        total = mix(mats_two[0], interp(regrouped, second_maps[0]))
        k = 1
        total = total + mix(mats_two[k], interp(regrouped, second_maps[k]))
        component = scale * total
        returned = lax.all_to_all(
            to_send_two(component, quarter), "mom", split_axis=0, concat_axis=1, tiled=True
        )
        state = source + from_send_two(returned, quarter)
    return (state, component)


def solution(mesh):
    placed = (
        P(("energy", "mom"), None, None),
        P(("energy", "mom"), None),
        P(),
        P(),
        P(),
        P(),
        P(),
        P(),
        P(),
        P(),
        P(),
        P(),
    )
    return jax.shard_map(
        shards,
        mesh=mesh,
        in_specs=placed,
        out_specs=(P(("energy", "mom"), None, None), P(("energy", "mom"), None, None)),
        check_vma=False,
    )
```

profile of v0, /device:TPU:1, one launch (start us, length us, event | category | flops | bytes accessed | tf_op | source)
XLA Modules:
  0.0 923.5 jit_solution(14042595359069601299)
XLA Ops:
  6.3 5.8 fusion.8
  12.2 4.1 fusion.14
  17.6 14.4 %fusion.68 = f32[8,128,1024]{2,1,0:T(8,128)S(1)} fusion(f32[8,128,1024]{2,1,0:T(8,128)S(1)} %fusion.8, f32[1024,1024,1]{0,1,2:T(8,128)S(1)} %bitcast.165), kind=kOutput, calls=%fused_computation.102 | convolution fusion | flops 12884901888 | bytes 12582912 | tf_op jit(solution)/shard_map/rcx,yx->rcy/dot_general | solution.py:43
  31.9 14.8 %convolution_add_fusion.1 = f32[8,128,1024]{2,1,0:T(8,128)} fusion(f32[8,128,1024]{2,1,0:T(8,128)S(1)} %fusion.68, f32[8,128,1024]{2,1,0:T(8,128)S(1)} %fusion.14, f32[1024,1024,1]{0,1,2:T(8,128)S(1)} %bitcast.156), kind=kOutput, calls=%fused_computation.13 | convolution fusion | flops 12885950464 | bytes 16777216 | tf_op jit(solution)/shard_map/rcx,yx->rcy/dot_general | solution.py:43
  46.8 11.6 %reshape.954 = f32[8,4,32,32,32]{4,3,2,1,0:T(8,128)} reshape(f32[8,128,1024]{2,1,0:T(8,128)} %convolution_add_fusion.1) | data formatting | bytes 8388608 | tf_op jit(solution)/shard_map/reshape | solution.py:49
  58.4 14.3 %copy.127 = f32[8,4,32,32,32]{4,2,0,1,3:T(8,128)} copy(f32[8,4,32,32,32]{4,3,2,1,0:T(8,128)} %reshape.954) | data formatting | bytes 8388608 | tf_op jit(solution)/shard_map/reshape | solution.py:49
  72.7 13.7 %reshape.955 = f32[128,8,1024]{2,1,0:T(8,128)} reshape(f32[32,4,8,32,32]{4,3,2,1,0:T(8,128)} %bitcast.148) | data formatting | bytes 8388608 | tf_op jit(solution)/shard_map/reshape | solution.py:51
  86.4 7.5 all-to-all-start
  97.9 2.6 broadcast_multiply_fusion
  100.5 71.5 %all-to-all-done = f32[128,8,1024]{2,1,0:T(8,128)} async-done(((f32[128,8,1024]{2,1,0:T(8,128)}), f32[128,8,1024]{2,1,0:T(8,128)}, u32[]{:S(2)}, u32[]{:S(2)}) %all-to-all-start) | async-done | bytes 4194336 | tf_op jit(solution)/shard_map/all_to_all | solution.py:117
  172.0 4.8 copy.131
  176.8 11.6 %reshape.956 = f32[8,32,4,32,32]{4,3,2,1,0:T(8,128)} reshape(f32[8,16,8,1024]{3,2,1,0:T(8,128)} %bitcast.158) | data formatting | bytes 8388608 | tf_op jit(solution)/shard_map/reshape | solution.py:58
  188.4 18.9 %copy.53 = f32[8,32,4,32,32]{4,3,2,1,0:T(8,128)} copy(f32[8,32,4,32,32]{3,1,2,4,0:T(8,128)} %bitcast.149) | data formatting | bytes 8388608 | tf_op jit(solution)/shard_map/transpose | solution.py:59
  207.3 13.7 %reshape.957 = f32[8,128,1024]{2,1,0:T(8,128)} reshape(f32[8,32,4,32,32]{4,3,2,1,0:T(8,128)} %copy.53) | data formatting | bytes 8388608 | tf_op jit(solution)/shard_map/reshape | solution.py:60
  221.0 17.2 %fusion.70 = f32[8,128,1024]{2,1,0:T(8,128)S(1)} fusion(f32[8,128,1024]{2,1,0:T(8,128)} %reshape.957, f32[1024,1024,1]{0,1,2:T(8,128)} %bitcast.169), kind=kOutput, calls=%fused_computation.104 | convolution fusion | flops 12884901888 | bytes 12582912 | tf_op jit(solution)/shard_map/rcx,yx->rcy/dot_general | solution.py:43
  238.2 13.4 %fusion.69 = f32[8,128,1024]{2,1,0:T(8,128)S(1)} fusion(f32[8,128,1024]{2,1,0:T(8,128)S(1)} %copy-done.6, f32[1024,1024,1]{0,1,2:T(8,128)S(1)} %bitcast.167), kind=kOutput, calls=%fused_computation.103 | convolution fusion | flops 12884901888 | bytes 12582912 | tf_op jit(solution)/shard_map/rcx,yx->rcy/dot_general | solution.py:43
  251.7 4.2 fusion.4
  255.9 5.2 add_multiply_fusion.1
  261.2 11.6 %reshape.958 = f32[8,32,4,32,32]{4,3,2,1,0:T(8,128)} reshape(f32[8,128,1024]{2,1,0:T(8,128)} %add_multiply_fusion.1) | data formatting | bytes 8388608 | tf_op jit(solution)/shard_map/reshape | solution.py:67
  272.8 20.0 %copy.59 = f32[8,32,4,32,32]{3,1,0,2,4:T(8,128)} copy(f32[8,32,4,32,32]{4,3,2,1,0:T(8,128)} %reshape.958) | data formatting | bytes 8388608 | tf_op jit(solution)/shard_map/reshape | solution.py:67
  292.8 13.7 %reshape.959 = f32[128,8,1024]{2,1,0:T(8,128)} reshape(f32[32,4,8,32,32]{4,3,2,1,0:T(8,128)} %bitcast.150) | data formatting | bytes 8388608 | tf_op jit(solution)/shard_map/reshape | solution.py:69
  306.5 111.9 %all_to_all.60 = f32[128,8,1024]{2,1,0:T(8,128)S(1)} all-to-all(f32[128,8,1024]{2,1,0:T(8,128)} %reshape.959), channel_id=1, replica_groups=mesh['energy'=2,'mom'=16] {'mom'}, dimensions={0} | all-to-all | bytes 8388608 | tf_op jit(solution)/shard_map/all_to_all | solution.py:125
  420.7 11.6 %reshape.960 = f32[8,32,4,32,32]{4,3,2,1,0:T(8,128)} reshape(f32[8,16,8,1024]{3,2,1,0:T(8,128)} %bitcast.159) | data formatting | bytes 8388608 | tf_op jit(solution)/shard_map/reshape | solution.py:76
  432.3 18.4 %copy.61 = f32[8,4,32,32,32]{4,3,2,1,0:T(8,128)} copy(f32[8,4,32,32,32]{4,2,1,3,0:T(8,128)} %bitcast.151) | data formatting | bytes 8388608 | tf_op jit(solution)/shard_map/transpose | solution.py:77
  450.8 13.7 %reshape.961 = f32[8,128,1024]{2,1,0:T(8,128)} reshape(f32[8,4,32,32,32]{4,3,2,1,0:T(8,128)} %copy.61) | data formatting | bytes 8388608 | tf_op jit(solution)/shard_map/reshape | solution.py:78
  464.4 6.4 fusion
  470.8 3.9 fusion.2
  474.8 14.2 %fusion.71 = f32[8,128,1024]{2,1,0:T(8,128)S(1)} fusion(f32[8,128,1024]{2,1,0:T(8,128)S(1)} %fusion.2, f32[1024,1024,1]{0,1,2:T(8,128)S(1)} %bitcast.166), kind=kOutput, calls=%fused_computation.105 | convolution fusion | flops 12884901888 | bytes 12582912 | tf_op jit(solution)/shard_map/rcx,yx->rcy/dot_general | solution.py:43
  489.0 14.8 %convolution_add_fusion = f32[8,128,1024]{2,1,0:T(8,128)} fusion(f32[8,128,1024]{2,1,0:T(8,128)S(1)} %fusion.71, f32[8,128,1024]{2,1,0:T(8,128)S(1)} %fusion, f32[1024,1024,1]{0,1,2:T(8,128)S(1)} %bitcast.157), kind=kOutput, calls=%fused_computation.12 | convolution fusion | flops 12885950464 | bytes 16777216 | tf_op jit(solution)/shard_map/rcx,yx->rcy/dot_general | solution.py:43
  503.8 11.6 %reshape.962 = f32[8,4,32,32,32]{4,3,2,1,0:T(8,128)} reshape(f32[8,128,1024]{2,1,0:T(8,128)} %convolution_add_fusion) | data formatting | bytes 8388608 | tf_op jit(solution)/shard_map/reshape | solution.py:49
  515.4 14.3 %copy.126 = f32[8,4,32,32,32]{4,2,0,1,3:T(8,128)} copy(f32[8,4,32,32,32]{4,3,2,1,0:T(8,128)} %reshape.962) | data formatting | bytes 8388608 | tf_op jit(solution)/shard_map/reshape | solution.py:49
  529.7 13.7 %reshape.963 = f32[128,8,1024]{2,1,0:T(8,128)} reshape(f32[32,4,8,32,32]{4,3,2,1,0:T(8,128)} %bitcast.152) | data formatting | bytes 8388608 | tf_op jit(solution)/shard_map/reshape | solution.py:51
  543.4 97.4 %all_to_all.61 = f32[128,8,1024]{2,1,0:T(8,128)S(1)} all-to-all(f32[128,8,1024]{2,1,0:T(8,128)} %reshape.963), channel_id=1, replica_groups=mesh['energy'=2,'mom'=16] {'mom'}, dimensions={0} | all-to-all | bytes 8388608 | tf_op jit(solution)/shard_map/all_to_all | solution.py:117
  643.1 11.6 %reshape.964 = f32[8,32,4,32,32]{4,3,2,1,0:T(8,128)} reshape(f32[8,16,8,1024]{3,2,1,0:T(8,128)} %bitcast.160) | data formatting | bytes 8388608 | tf_op jit(solution)/shard_map/reshape | solution.py:58
  654.7 18.9 %copy.68 = f32[8,32,4,32,32]{4,3,2,1,0:T(8,128)} copy(f32[8,32,4,32,32]{3,1,2,4,0:T(8,128)} %bitcast.153) | data formatting | bytes 8388608 | tf_op jit(solution)/shard_map/transpose | solution.py:59
  673.6 13.7 %reshape.965 = f32[8,128,1024]{2,1,0:T(8,128)} reshape(f32[8,32,4,32,32]{4,3,2,1,0:T(8,128)} %copy.68) | data formatting | bytes 8388608 | tf_op jit(solution)/shard_map/reshape | solution.py:60
  687.3 17.2 %fusion.73 = f32[8,128,1024]{2,1,0:T(8,128)S(1)} fusion(f32[8,128,1024]{2,1,0:T(8,128)} %reshape.965, f32[1024,1024,1]{0,1,2:T(8,128)} %bitcast.170), kind=kOutput, calls=%fused_computation.107 | convolution fusion | flops 12884901888 | bytes 12582912 | tf_op jit(solution)/shard_map/rcx,yx->rcy/dot_general | solution.py:43
  704.6 13.4 %fusion.72 = f32[8,128,1024]{2,1,0:T(8,128)S(1)} fusion(f32[8,128,1024]{2,1,0:T(8,128)S(1)} %copy-done.5, f32[1024,1024,1]{0,1,2:T(8,128)S(1)} %bitcast.168), kind=kOutput, calls=%fused_computation.106 | convolution fusion | flops 12884901888 | bytes 12582912 | tf_op jit(solution)/shard_map/rcx,yx->rcy/dot_general | solution.py:43
  718.0 4.2 fusion.6
  722.3 5.2 add_multiply_fusion
  727.5 11.6 %reshape.966 = f32[8,32,4,32,32]{4,3,2,1,0:T(8,128)} reshape(f32[8,128,1024]{2,1,0:T(8,128)} %add_multiply_fusion) | data formatting | bytes 8388608 | tf_op jit(solution)/shard_map/reshape | solution.py:67
  739.1 20.0 %copy.73 = f32[8,32,4,32,32]{3,1,0,2,4:T(8,128)} copy(f32[8,32,4,32,32]{4,3,2,1,0:T(8,128)} %reshape.966) | data formatting | bytes 8388608 | tf_op jit(solution)/shard_map/reshape | solution.py:67
  759.1 13.7 %reshape.967 = f32[128,8,1024]{2,1,0:T(8,128)} reshape(f32[32,4,8,32,32]{4,3,2,1,0:T(8,128)} %bitcast.154) | data formatting | bytes 8388608 | tf_op jit(solution)/shard_map/reshape | solution.py:69
  772.8 97.6 %all_to_all.62 = f32[128,8,1024]{2,1,0:T(8,128)S(1)} all-to-all(f32[128,8,1024]{2,1,0:T(8,128)} %reshape.967), channel_id=1, replica_groups=mesh['energy'=2,'mom'=16] {'mom'}, dimensions={0} | all-to-all | bytes 8388608 | tf_op jit(solution)/shard_map/all_to_all | solution.py:125
  872.7 11.6 %reshape.968 = f32[8,32,4,32,32]{4,3,2,1,0:T(8,128)} reshape(f32[8,16,8,1024]{3,2,1,0:T(8,128)} %bitcast.161) | data formatting | bytes 8388608 | tf_op jit(solution)/shard_map/reshape | solution.py:76
  884.3 18.4 %copy.75 = f32[8,4,32,32,32]{4,3,2,1,0:T(8,128)} copy(f32[8,4,32,32,32]{4,2,1,3,0:T(8,128)} %bitcast.155) | data formatting | bytes 8388608 | tf_op jit(solution)/shard_map/transpose | solution.py:77
  902.8 13.7 %reshape.969 = f32[8,128,1024]{2,1,0:T(8,128)} reshape(f32[8,4,32,32,32]{4,3,2,1,0:T(8,128)} %copy.75) | data formatting | bytes 8388608 | tf_op jit(solution)/shard_map/reshape | solution.py:78
  916.4 6.8 add.250
  (59 shorter events, 17.9 us)
Async XLA Ops:
  6.3 5.8 copy-start
  16.9 15.0 %copy-start.7 = (f32[1024,32,32]{0,2,1:T(8,128)}, f32[1024,32,32]{0,2,1:T(8,128)S(1)}, u32[]{:S(2)}) copy-start(f32[1024,32,32]{0,2,1:T(8,128)S(1)} %broadcast_multiply_fusion.3) | copy-start | bytes 12582916
  17.5 14.4 %copy-start.3 = (f32[1024,32,32]{0,2,1:T(8,128)}, f32[1024,32,32]{0,2,1:T(8,128)S(1)}, u32[]{:S(2)}) copy-start(f32[1024,32,32]{0,2,1:T(8,128)S(1)} %broadcast_multiply_fusion.2) | copy-start | bytes 12582916
  86.3 7.5 copy-start.15
  86.3 7.5 copy-start.16
  86.3 7.6 copy-start.13
  86.3 7.6 copy-start.14
  86.4 7.9 copy-start.11
  86.4 85.6 %all-to-all-start = ((f32[128,8,1024]{2,1,0:T(8,128)}), f32[128,8,1024]{2,1,0:T(8,128)}, u32[]{:S(2)}, u32[]{:S(2)}) async-start(f32[128,8,1024]{2,1,0:T(8,128)} %reshape.955), calls=%async_computation | async-start | bytes 8388608 | tf_op jit(solution)/shard_map/all_to_all | solution.py:117
  221.0 17.2 %copy-start.6 = (f32[8,128,1024]{2,1,0:T(8,128)S(1)}, f32[8,128,1024]{2,1,0:T(8,128)}, u32[]{:S(2)}) copy-start(f32[8,128,1024]{2,1,0:T(8,128)} %reshape.957) | copy-start | bytes 12582916
  221.0 17.3 %copy-start.9 = (f32[1024,32,32]{0,2,1:T(8,128)S(1)}, f32[1024,32,32]{0,2,1:T(8,128)}, u32[]{:S(2)}) copy-start(f32[1024,32,32]{0,2,1:T(8,128)} %broadcast_multiply_fusion.1) | copy-start | bytes 12582916
  251.7 4.3 copy-start.12
  464.4 6.4 copy-start.1
  464.4 6.4 copy-start.2
  470.8 4.0 copy-start.8
  474.8 14.2 %copy-start.4 = (f32[1024,32,32]{0,2,1:T(8,128)S(1)}, f32[1024,32,32]{0,2,1:T(8,128)}, u32[]{:S(2)}) copy-start(f32[1024,32,32]{0,2,1:T(8,128)} %copy-done.3) | copy-start | bytes 12582916
  687.3 17.2 %copy-start.5 = (f32[8,128,1024]{2,1,0:T(8,128)S(1)}, f32[8,128,1024]{2,1,0:T(8,128)}, u32[]{:S(2)}) copy-start(f32[8,128,1024]{2,1,0:T(8,128)} %reshape.965) | copy-start | bytes 12582916
  687.3 17.3 %copy-start.10 = (f32[1024,32,32]{0,2,1:T(8,128)S(1)}, f32[1024,32,32]{0,2,1:T(8,128)}, u32[]{:S(2)}) copy-start(f32[1024,32,32]{0,2,1:T(8,128)} %broadcast_multiply_fusion.1) | copy-start | bytes 12582916
where the time goes:
time: 932 us; the launch traced here: 923 us
  local copies, waits for them, and re-layouts  362 us (39%)
  blocking collectives  307 us (33%)
  matrix products  161 us (17%)
  waiting for transfers between devices  71.5 us (8%)
  other arithmetic  13.5 us (1%)
    all_to_all x2, blocking collectives, shards(): lax.all_to_all(to_send_two(component, quarter), 'mom', split_axis=0, conc...  210 us
    dot_general x8, matrix products, interp(): jnp.einsum('rcx,yx->rcy', values, smat, precision=lax.Precision.HIGHEST)  120 us
    all_to_all x1, blocking collectives, shards(): lax.all_to_all(to_send_one(one, quarter), 'mom', split_axis=0, concat_axi...  97.4 us
    all_to_all x1, waiting for transfers between devices, shards(): lax.all_to_all(to_send_one(one, quarter), 'mom', split_axis=0, concat_axi...  71.5 us
    reshape x4, local copies, waits for them, and re-layouts, to_send_two(): values.reshape(rows, quarter, 4, Q, R).transpose(4, 2, 0, 1, 3)  63.2 us
    reshape x4, local copies, waits for them, and re-layouts, to_send_one(): values.reshape(rows, 4, quarter, P_SIZE, Q).transpose(3, 1, 0, 2, 4)  51.8 us
    dot_general x8, matrix products, mix(): jnp.einsum('rmn,rnx->rmx', mats, values, precision=lax.Precision.HIGHEST)  39.1 us
    transpose x2, local copies, waits for them, and re-layouts, from_send_one(): return arrived.reshape(rows, R, 4, quarter, Q).transpose(0, 3, 2, 4, 1).r...  37.8 us
  transfers between devices with their start and end apart: 1, of which 1 were waited for; matrix products, arithmetic and copies ran while one was open for 1% of the time, Pallas kernels for 0%

commit v1 on v0

--- a/solution.py
+++ b/solution.py
@@ -2,6 +2,7 @@
 import jax.numpy as jnp
 from jax import lax
 from jax.sharding import PartitionSpec as P
+from jax.lax import all_to_all, axis_size
 
 P_SIZE = 32
 Q = 32
@@ -114,9 +115,14 @@
         one = interp(mix(mats_one[0], state), first_maps[0])
         k = 1
         one = one + interp(mix(mats_one[k], state), first_maps[k])
-        arrived = lax.all_to_all(
-            to_send_one(one, quarter), "mom", split_axis=0, concat_axis=1, tiled=True
-        )
+
+        def set_tiles(mine_x, d0, d_out):
+            return jnp.concatenate(
+                all_to_all(jnp.stack(jnp.split(mine_x, axis_size("mom"), axis=d0)), "mom", 0, 0),
+                axis=d_out,
+            )
+
+        arrived = set_tiles(to_send_one(one, quarter), 0, 1)
         regrouped = from_send_one(arrived, quarter)
         total = mix(mats_two[0], interp(regrouped, second_maps[0]))
         k = 1

time: 932 us -> 1020 us (1.094)
  local copies, waits for them, and re-layouts: 362 us -> 445 us
    another operation x0 -> x36, local copies, waits for them, and re-layouts: none -> 93.1 us  [the longest x34 69.9 us: set_tiles(): jnp.stack(jnp.split(mine_x, axis_size('mom'), axis=d0))]
    reshape x4 -> x2, local copies, waits for them, and re-layouts: 50.6 us -> 7.11 us  [set_tiles(): jnp.concatenate(all_to_all(jnp.stack(jnp.split(mine_x, axis_size('mom'),...]
    unnamed x34 -> x84, local copies, waits for them, and re-layouts: 0.07 us -> 39 us
    split x0 -> x2, local copies, waits for them, and re-layouts: none -> 10.5 us  [set_tiles(): jnp.split(mine_x, axis_size('mom'), axis=d0)]
where the time goes in v1:
time: 1020 us; the launch traced here: 1010 us
  local copies, waits for them, and re-layouts  445 us (44%)
  blocking collectives  307 us (30%)
  matrix products  160 us (16%)
  waiting for transfers between devices  71.3 us (7%)
  other arithmetic  13.5 us (1%)
    all_to_all x2, blocking collectives, shards(): lax.all_to_all(to_send_two(component, quarter), 'mom', split_axis=0, conc...  210 us
    dot_general x8, matrix products, interp(): jnp.einsum('rcx,yx->rcy', values, smat, precision=lax.Precision.HIGHEST)  119 us
    all_to_all x1, blocking collectives, set_tiles(): all_to_all(jnp.stack(jnp.split(mine_x, axis_size('mom'), axis=d0)), 'mom'...  97.6 us
    all_to_all x1, waiting for transfers between devices, set_tiles(): all_to_all(jnp.stack(jnp.split(mine_x, axis_size('mom'), axis=d0)), 'mom'...  71.3 us
    another operation x34, local copies, waits for them, and re-layouts, set_tiles(): jnp.stack(jnp.split(mine_x, axis_size('mom'), axis=d0))  69.9 us
    reshape x4, local copies, waits for them, and re-layouts, to_send_two(): values.reshape(rows, quarter, 4, Q, R).transpose(4, 2, 0, 1, 3)  63.3 us
    reshape x4, local copies, waits for them, and re-layouts, to_send_one(): values.reshape(rows, 4, quarter, P_SIZE, Q).transpose(3, 1, 0, 2, 4)  42.6 us
    unnamed x84, local copies, waits for them, and re-layouts  39 us
  transfers between devices with their start and end apart: 1, of which 1 were waited for; matrix products, arithmetic and copies ran while one was open for 1% of the time, Pallas kernels for 0%

profile of v1, /device:TPU:1, one launch (start us, length us, event | category | flops | bytes accessed | tf_op | source)
XLA Modules:
  0.0 1006.2 jit_solution(8085703493979798703)
XLA Ops:
  6.3 5.7 fusion.8
  12.0 4.1 fusion.14
  16.8 14.0 %fusion.70 = f32[8,128,1024]{2,1,0:T(8,128)S(1)} fusion(f32[8,128,1024]{2,1,0:T(8,128)S(1)} %fusion.8, f32[1024,1024,1]{0,1,2:T(8,128)S(1)} %bitcast.217), kind=kOutput, calls=%fused_computation.134 | convolution fusion | flops 12884901888 | bytes 12582912 | tf_op jit(solution)/shard_map/rcx,yx->rcy/dot_general | solution.py:44
  33.4 14.8 %convolution_add_fusion.1 = f32[8,128,1024]{2,1,0:T(8,128)} fusion(f32[8,128,1024]{2,1,0:T(8,128)S(1)} %fusion.70, f32[8,128,1024]{2,1,0:T(8,128)S(1)} %fusion.14, f32[1024,1024,1]{0,1,2:T(8,128)S(1)} %bitcast.210), kind=kOutput, calls=%fused_computation.11 | convolution fusion | flops 12885950464 | bytes 16777216 | tf_op jit(solution)/shard_map/rcx,yx->rcy/dot_general | solution.py:44
  48.2 11.6 %reshape.1012 = f32[8,4,32,32,32]{4,3,2,1,0:T(8,128)} reshape(f32[8,128,1024]{2,1,0:T(8,128)} %convolution_add_fusion.1) | data formatting | bytes 8388608 | tf_op jit(solution)/shard_map/reshape | solution.py:50
  59.8 9.8 copy.125
  69.6 5.3 fusion.59
  128.4 7.8 all-to-all-start
  140.2 2.6 broadcast_multiply_fusion
  142.8 71.3 %all-to-all-done = f32[16,8,8,1024]{3,2,1,0:T(8,128)} async-done(((f32[16,8,8,1024]{3,2,1,0:T(8,128)}), f32[16,8,8,1024]{3,2,1,0:T(8,128)}, u32[]{:S(2)}, u32[]{:S(2)}) %all-to-all-start) | async-done | bytes 4194336 | tf_op jit(solution)/shard_map/all_to_all | solution.py:121
  214.1 4.8 copy.52
  218.9 11.6 %reshape_reshape.6 = f32[8,32,4,32,32]{4,3,2,1,0:T(8,128)} reshape(f32[8,16,8,1024]{3,2,1,0:T(8,128)} %copy.52) | data formatting | bytes 8388608 | tf_op jit(solution)/shard_map/reshape;reshape | solution.py:59
  230.6 18.9 %copy.53 = f32[8,32,4,32,32]{4,3,2,1,0:T(8,128)} copy(f32[8,32,4,32,32]{3,1,2,4,0:T(8,128)} %bitcast.202) | data formatting | bytes 8388608 | tf_op jit(solution)/shard_map/transpose | solution.py:60
  249.4 13.7 %reshape.1014 = f32[8,128,1024]{2,1,0:T(8,128)} reshape(f32[8,32,4,32,32]{4,3,2,1,0:T(8,128)} %copy.53) | data formatting | bytes 8388608 | tf_op jit(solution)/shard_map/reshape | solution.py:61
  263.1 17.2 %fusion.71 = f32[8,128,1024]{2,1,0:T(8,128)S(1)} fusion(f32[8,128,1024]{2,1,0:T(8,128)} %reshape.1014, f32[1024,1024,1]{0,1,2:T(8,128)} %bitcast.219), kind=kOutput, calls=%fused_computation.135 | convolution fusion | flops 12884901888 | bytes 12582912 | tf_op jit(solution)/shard_map/rcx,yx->rcy/dot_general | solution.py:44
  280.4 13.4 %fusion.72 = f32[8,128,1024]{2,1,0:T(8,128)S(1)} fusion(f32[8,128,1024]{2,1,0:T(8,128)S(1)} %copy-done.6, f32[1024,1024,1]{0,1,2:T(8,128)S(1)} %bitcast.222), kind=kOutput, calls=%fused_computation.136 | convolution fusion | flops 12884901888 | bytes 12582912 | tf_op jit(solution)/shard_map/rcx,yx->rcy/dot_general | solution.py:44
  293.8 4.2 fusion.4
  298.1 5.2 add_multiply_fusion.1
  303.3 11.6 %reshape.1015 = f32[8,32,4,32,32]{4,3,2,1,0:T(8,128)} reshape(f32[8,128,1024]{2,1,0:T(8,128)} %add_multiply_fusion.1) | data formatting | bytes 8388608 | tf_op jit(solution)/shard_map/reshape | solution.py:68
  314.9 20.0 %copy.59 = f32[8,32,4,32,32]{3,1,0,2,4:T(8,128)} copy(f32[8,32,4,32,32]{4,3,2,1,0:T(8,128)} %reshape.1015) | data formatting | bytes 8388608 | tf_op jit(solution)/shard_map/reshape | solution.py:68
  334.9 13.7 %reshape.1016 = f32[128,8,1024]{2,1,0:T(8,128)} reshape(f32[32,4,8,32,32]{4,3,2,1,0:T(8,128)} %bitcast.203) | data formatting | bytes 8388608 | tf_op jit(solution)/shard_map/reshape | solution.py:70
  348.6 111.9 %all_to_all.40 = f32[128,8,1024]{2,1,0:T(8,128)S(1)} all-to-all(f32[128,8,1024]{2,1,0:T(8,128)} %reshape.1016), channel_id=1, replica_groups=mesh['energy'=2,'mom'=16] {'mom'}, dimensions={0} | all-to-all | bytes 8388608 | tf_op jit(solution)/shard_map/all_to_all | solution.py:131
  462.8 11.6 %reshape.1017 = f32[8,32,4,32,32]{4,3,2,1,0:T(8,128)} reshape(f32[8,16,8,1024]{3,2,1,0:T(8,128)} %bitcast.212) | data formatting | bytes 8388608 | tf_op jit(solution)/shard_map/reshape | solution.py:77
  474.4 18.5 %copy.61 = f32[8,4,32,32,32]{4,3,2,1,0:T(8,128)} copy(f32[8,4,32,32,32]{4,2,1,3,0:T(8,128)} %bitcast.204) | data formatting | bytes 8388608 | tf_op jit(solution)/shard_map/transpose | solution.py:78
  492.9 13.7 %reshape.1018 = f32[8,128,1024]{2,1,0:T(8,128)} reshape(f32[8,4,32,32,32]{4,3,2,1,0:T(8,128)} %copy.61) | data formatting | bytes 8388608 | tf_op jit(solution)/shard_map/reshape | solution.py:79
  506.6 6.4 fusion.2
  513.0 3.9 fusion
  516.9 14.2 %fusion.73 = f32[8,128,1024]{2,1,0:T(8,128)S(1)} fusion(f32[8,128,1024]{2,1,0:T(8,128)S(1)} %fusion.2, f32[1024,1024,1]{0,1,2:T(8,128)S(1)} %bitcast.218), kind=kOutput, calls=%fused_computation.137 | convolution fusion | flops 12884901888 | bytes 12582912 | tf_op jit(solution)/shard_map/rcx,yx->rcy/dot_general | solution.py:44
  531.1 14.8 %convolution_add_fusion = f32[8,128,1024]{2,1,0:T(8,128)} fusion(f32[8,128,1024]{2,1,0:T(8,128)S(1)} %fusion.73, f32[8,128,1024]{2,1,0:T(8,128)S(1)} %fusion, f32[1024,1024,1]{0,1,2:T(8,128)S(1)} %bitcast.211), kind=kOutput, calls=%fused_computation.10 | convolution fusion | flops 12885950464 | bytes 16777216 | tf_op jit(solution)/shard_map/rcx,yx->rcy/dot_general | solution.py:44
  546.0 11.6 %reshape.1019 = f32[8,4,32,32,32]{4,3,2,1,0:T(8,128)} reshape(f32[8,128,1024]{2,1,0:T(8,128)} %convolution_add_fusion) | data formatting | bytes 8388608 | tf_op jit(solution)/shard_map/reshape | solution.py:50
  557.6 9.6 copy.124
  567.1 5.3 fusion.58
  625.9 97.6 %all_to_all.41 = f32[16,8,8,1024]{3,2,1,0:T(8,128)S(1)} all-to-all(f32[16,8,8,1024]{3,2,1,0:T(8,128)} %constant_dynamic-update-slice_fusion.16), channel_id=1, replica_groups=mesh['energy'=2,'mom'=16] {'mom'}, dimensions={0} | all-to-all | bytes 8388608 | tf_op jit(solution)/shard_map/all_to_all | solution.py:121
  725.8 11.6 %reshape_reshape.7 = f32[8,32,4,32,32]{4,3,2,1,0:T(8,128)} reshape(f32[8,16,8,1024]{3,2,1,0:T(8,128)} %copy.67) | data formatting | bytes 8388608 | tf_op jit(solution)/shard_map/reshape;reshape | solution.py:59
  737.5 18.9 %copy.68 = f32[8,32,4,32,32]{4,3,2,1,0:T(8,128)} copy(f32[8,32,4,32,32]{3,1,2,4,0:T(8,128)} %bitcast.205) | data formatting | bytes 8388608 | tf_op jit(solution)/shard_map/transpose | solution.py:60
  756.3 13.7 %reshape.1021 = f32[8,128,1024]{2,1,0:T(8,128)} reshape(f32[8,32,4,32,32]{4,3,2,1,0:T(8,128)} %copy.68) | data formatting | bytes 8388608 | tf_op jit(solution)/shard_map/reshape | solution.py:61
  770.0 17.4 %fusion.75 = f32[8,128,1024]{2,1,0:T(8,128)S(1)} fusion(f32[8,128,1024]{2,1,0:T(8,128)} %reshape.1021, f32[1024,1024,1]{0,1,2:T(8,128)} %bitcast.221), kind=kOutput, calls=%fused_computation.139 | convolution fusion | flops 12884901888 | bytes 12582912 | tf_op jit(solution)/shard_map/rcx,yx->rcy/dot_general | solution.py:44
  787.5 13.4 %fusion.74 = f32[8,128,1024]{2,1,0:T(8,128)S(1)} fusion(f32[8,128,1024]{2,1,0:T(8,128)S(1)} %copy-done.5, f32[1024,1024,1]{0,1,2:T(8,128)S(1)} %bitcast.220), kind=kOutput, calls=%fused_computation.138 | convolution fusion | flops 12884901888 | bytes 12582912 | tf_op jit(solution)/shard_map/rcx,yx->rcy/dot_general | solution.py:44
  800.9 4.0 fusion.6
  804.9 5.2 add_multiply_fusion
  810.1 11.6 %reshape.1022 = f32[8,32,4,32,32]{4,3,2,1,0:T(8,128)} reshape(f32[8,128,1024]{2,1,0:T(8,128)} %add_multiply_fusion) | data formatting | bytes 8388608 | tf_op jit(solution)/shard_map/reshape | solution.py:68
  821.8 20.0 %copy.73 = f32[8,32,4,32,32]{3,1,0,2,4:T(8,128)} copy(f32[8,32,4,32,32]{4,3,2,1,0:T(8,128)} %reshape.1022) | data formatting | bytes 8388608 | tf_op jit(solution)/shard_map/reshape | solution.py:68
  841.8 13.7 %reshape.1023 = f32[128,8,1024]{2,1,0:T(8,128)} reshape(f32[32,4,8,32,32]{4,3,2,1,0:T(8,128)} %bitcast.206) | data formatting | bytes 8388608 | tf_op jit(solution)/shard_map/reshape | solution.py:70
  855.4 97.6 %all_to_all.42 = f32[128,8,1024]{2,1,0:T(8,128)S(1)} all-to-all(f32[128,8,1024]{2,1,0:T(8,128)} %reshape.1023), channel_id=1, replica_groups=mesh['energy'=2,'mom'=16] {'mom'}, dimensions={0} | all-to-all | bytes 8388608 | tf_op jit(solution)/shard_map/all_to_all | solution.py:131
  955.4 11.6 %reshape.1024 = f32[8,32,4,32,32]{4,3,2,1,0:T(8,128)} reshape(f32[8,16,8,1024]{3,2,1,0:T(8,128)} %bitcast.213) | data formatting | bytes 8388608 | tf_op jit(solution)/shard_map/reshape | solution.py:77
  967.0 18.5 %copy.75 = f32[8,4,32,32,32]{4,3,2,1,0:T(8,128)} copy(f32[8,4,32,32,32]{4,2,1,3,0:T(8,128)} %bitcast.207) | data formatting | bytes 8388608 | tf_op jit(solution)/shard_map/transpose | solution.py:78
  985.5 13.7 %reshape.1025 = f32[8,128,1024]{2,1,0:T(8,128)} reshape(f32[8,4,32,32,32]{4,3,2,1,0:T(8,128)} %copy.75) | data formatting | bytes 8388608 | tf_op jit(solution)/shard_map/reshape | solution.py:79
  999.1 6.8 add.250
  (143 shorter events, 126.7 us)
Async XLA Ops:
  6.3 5.7 copy-start
  16.8 14.0 %copy-start.7 = (f32[1024,32,32]{0,2,1:T(8,128)}, f32[1024,32,32]{0,2,1:T(8,128)S(1)}, u32[]{:S(2)}) copy-start(f32[1024,32,32]{0,2,1:T(8,128)S(1)} %broadcast_multiply_fusion.3) | copy-start | bytes 12582916
  31.4 2.0 copy-start.3
  109.3 15.4 %copy-start.15 = (f32[1,8,8,1024]{3,2,1,0:T(8,128)S(1)}, f32[1,8,8,1024]{3,2,1,0:T(8,128)}, u32[]{:S(2)}) copy-start(f32[1,8,8,1024]{3,2,1,0:T(8,128)} %stack.113) | copy-start | bytes 786436
  109.3 16.1 %copy-start.13 = (f32[1,8,8,1024]{3,2,1,0:T(8,128)S(1)}, f32[1,8,8,1024]{3,2,1,0:T(8,128)}, u32[]{:S(2)}) copy-start(f32[1,8,8,1024]{3,2,1,0:T(8,128)} %stack.114) | copy-start | bytes 786436
  109.3 16.8 %copy-start.11 = (f32[1,8,8,1024]{3,2,1,0:T(8,128)S(1)}, f32[1,8,8,1024]{3,2,1,0:T(8,128)}, u32[]{:S(2)}) copy-start(f32[1,8,8,1024]{3,2,1,0:T(8,128)} %stack.115) | copy-start | bytes 786436
  109.8 13.4 %copy-start.19 = (f32[1,8,8,1024]{3,2,1,0:T(8,128)S(1)}, f32[1,8,8,1024]{3,2,1,0:T(8,128)}, u32[]{:S(2)}) copy-start(f32[1,8,8,1024]{3,2,1,0:T(8,128)} %stack.111) | copy-start | bytes 786436
  109.8 14.2 %copy-start.17 = (f32[1,8,8,1024]{3,2,1,0:T(8,128)S(1)}, f32[1,8,8,1024]{3,2,1,0:T(8,128)}, u32[]{:S(2)}) copy-start(f32[1,8,8,1024]{3,2,1,0:T(8,128)} %stack.112) | copy-start | bytes 786436
  128.3 7.8 copy-start.25
  128.3 7.9 copy-start.26
  128.3 7.9 copy-start.23
  128.3 7.9 copy-start.24
  128.3 8.2 copy-start.21
  128.4 85.8 %all-to-all-start = ((f32[16,8,8,1024]{3,2,1,0:T(8,128)}), f32[16,8,8,1024]{3,2,1,0:T(8,128)}, u32[]{:S(2)}, u32[]{:S(2)}) async-start(f32[16,8,8,1024]{3,2,1,0:T(8,128)} %constant_dynamic-update-slice_fusion), calls=%async_computation | async-start | bytes 8388608 | tf_op jit(solution)/shard_map/all_to_all | solution.py:121
  263.1 17.2 %copy-start.6 = (f32[8,128,1024]{2,1,0:T(8,128)S(1)}, f32[8,128,1024]{2,1,0:T(8,128)}, u32[]{:S(2)}) copy-start(f32[8,128,1024]{2,1,0:T(8,128)} %reshape.1014) | copy-start | bytes 12582916
  263.1 17.3 %copy-start.10 = (f32[1024,32,32]{0,2,1:T(8,128)S(1)}, f32[1024,32,32]{0,2,1:T(8,128)}, u32[]{:S(2)}) copy-start(f32[1024,32,32]{0,2,1:T(8,128)} %broadcast_multiply_fusion) | copy-start | bytes 12582916
  293.8 4.3 copy-start.22
  506.6 6.4 copy-start.1
  506.6 6.4 copy-start.2
  513.0 4.0 copy-start.8
  516.9 14.2 %copy-start.4 = (f32[1024,32,32]{0,2,1:T(8,128)S(1)}, f32[1024,32,32]{0,2,1:T(8,128)}, u32[]{:S(2)}) copy-start(f32[1024,32,32]{0,2,1:T(8,128)} %copy-done.3) | copy-start | bytes 12582916
  606.9 15.4 %copy-start.16 = (f32[1,8,8,1024]{3,2,1,0:T(8,128)S(1)}, f32[1,8,8,1024]{3,2,1,0:T(8,128)}, u32[]{:S(2)}) copy-start(f32[1,8,8,1024]{3,2,1,0:T(8,128)} %stack.130) | copy-start | bytes 786436
  606.9 16.1 %copy-start.14 = (f32[1,8,8,1024]{3,2,1,0:T(8,128)S(1)}, f32[1,8,8,1024]{3,2,1,0:T(8,128)}, u32[]{:S(2)}) copy-start(f32[1,8,8,1024]{3,2,1,0:T(8,128)} %stack.131) | copy-start | bytes 786436
  606.9 16.8 %copy-start.12 = (f32[1,8,8,1024]{3,2,1,0:T(8,128)S(1)}, f32[1,8,8,1024]{3,2,1,0:T(8,128)}, u32[]{:S(2)}) copy-start(f32[1,8,8,1024]{3,2,1,0:T(8,128)} %stack.132) | copy-start | bytes 786436
  607.4 13.4 %copy-start.20 = (f32[1,8,8,1024]{3,2,1,0:T(8,128)S(1)}, f32[1,8,8,1024]{3,2,1,0:T(8,128)}, u32[]{:S(2)}) copy-start(f32[1,8,8,1024]{3,2,1,0:T(8,128)} %stack.128) | copy-start | bytes 786436
  607.4 14.2 %copy-start.18 = (f32[1,8,8,1024]{3,2,1,0:T(8,128)S(1)}, f32[1,8,8,1024]{3,2,1,0:T(8,128)}, u32[]{:S(2)}) copy-start(f32[1,8,8,1024]{3,2,1,0:T(8,128)} %stack.129) | copy-start | bytes 786436
  770.0 17.4 %copy-start.5 = (f32[8,128,1024]{2,1,0:T(8,128)S(1)}, f32[8,128,1024]{2,1,0:T(8,128)}, u32[]{:S(2)}) copy-start(f32[8,128,1024]{2,1,0:T(8,128)} %reshape.1021) | copy-start | bytes 12582916
  770.0 17.4 %copy-start.9 = (f32[1024,32,32]{0,2,1:T(8,128)S(1)}, f32[1024,32,32]{0,2,1:T(8,128)}, u32[]{:S(2)}) copy-start(f32[1024,32,32]{0,2,1:T(8,128)} %broadcast_multiply_fusion.1) | copy-start | bytes 12582916
